TPU v7x, 32 devices: a whole 2x2x4 slice. The times are simulated.
32 devices in a mesh: groups: 2 (over x), row: 16 (over z, y, core).
Axes of the slice: x: 2, y: 2, z: 4, core: 2. Of those that a mesh axis runs over, the one named last changes fastest.
Arguments:
- design_matrix: bfloat16 [1024, 65536], P('groups', 'row'), parts along dimension 0, may hold values from -0.0546875 to 0.0546875
- targets: float32 [1024, 128], P(('groups', 'row')), parts along dimension 0, may hold values from -24 to 24
- linear: float32 [131072, 128], P(('groups', 'row')), parts along dimension 0, may hold values from -24 to 24
- diagonal: float32 [131072], P(('groups', 'row')), parts along dimension 0, may hold values from 0.1 to 2
- lower_code: int32 [131072, 128], P(('groups', 'row')), parts along dimension 0, may hold values from -192 to -17
- upper_code: int32 [131072, 128], P(('groups', 'row')), parts along dimension 0, may hold values from 16 to 191
Outputs:
- box_iterate: float32 [131072, 128], P(('groups', 'row')), parts along dimension 0
- scaled_dual: float32 [131072, 128], P(('groups', 'row')), parts along dimension 0
There are 2 independent parts, one for each index of `groups`. A program takes and returns all parts, laid end to end along the dimension named above; each array names one. Nothing has to cross between parts.
All inputs are finite; a program needn't handle non-finite values.
Results may differ from a plain program's by a relative error of at most 0.00033.
Values may be sent and summed in bfloat16 or wider, within the bound.
A program may use at most 128 MiB of HBM per device.

v0:
```python
import jax
import jax.numpy as jnp
from jax import lax
from jax.sharding import PartitionSpec as P

ITERS = 4


rho_plus_lip = 7.0


def solve_small(matrix, rhs):
    count = len(rhs)
    table = [list(line) for line in matrix]
    right = list(rhs)
    for p in range(count):
        for i in range(p + 1, count):
            factor = table[i][p] / table[p][p]
            for j in range(p, count):
                table[i][j] = table[i][j] - factor * table[p][j]
            right[i] = right[i] - factor * right[p]
    result = [None] * count
    for i in reversed(range(count)):
        total = right[i]
        for j in range(i + 1, count):
            total = total - table[i][j] * result[j]
        result[i] = total / table[i][i]
    return result


def mix_weights(gram):
    count = len(gram)
    trace = gram[0][0]
    for i in range(1, count):
        trace = trace + gram[i][i]
    shift = 0.01 * trace / count + 1e-06
    matrix = [[gram[i][j] + (shift if i == j else 0.0) for j in range(count)] for i in range(count)]
    solved = solve_small(matrix, [jnp.ones_like(trace)] * count)
    total = solved[0]
    for i in range(1, count):
        total = total + solved[i]
    return [item / total for item in solved]


def per_device(design_matrix, targets, linear, diagonal, lower_code, upper_code):
    lower = lower_code.astype(jnp.float32) / 64.0
    upper = upper_code.astype(jnp.float32) / 64.0
    step_size = (1.0 / (rho_plus_lip + diagonal))[:, None]
    state = jnp.zeros((2,) + linear.shape, jnp.float32)
    hist_mapped = []
    hist_change = []
    gram = []
    for iteration in range(ITERS):
        point = state[0] - state[1]
        point_b = point.astype(jnp.bfloat16)
        product = lax.psum_scatter(
            jnp.dot(design_matrix, point_b, preferred_element_type=jnp.float32),
            "row",
            scatter_dimension=0,
            tiled=True,
        )
        misfit = (product - targets).astype(jnp.bfloat16)
        gradient = lax.dot_general(
            design_matrix,
            lax.all_gather(misfit, "row", axis=0, tiled=True),
            (((0,), (0,)), ((), ())),
            preferred_element_type=jnp.float32,
        )
        gradient = gradient + diagonal[:, None] * point + linear
        moved = point - step_size * gradient
        boxed = jnp.clip(moved + state[1], lower, upper)
        scaled = state[1] + moved - boxed
        mapped = jnp.stack([boxed, scaled])
        change = mapped - state
        hist_mapped.append(mapped)
        hist_change.append(change)
        count = len(hist_change)
        stacked = jnp.stack(hist_change)
        partial_all = jnp.einsum(
            "icns,jcns->ijs", stacked, stacked, precision=lax.Precision.HIGHEST
        )
        whole = lax.psum(partial_all, "row")
        gram = [[whole[i, j] for j in range(count)] for i in range(count)]
        alpha = mix_weights(gram)
        combined = alpha[0][None, None, :] * hist_mapped[0]
        for i in range(1, count):
            combined = combined + alpha[i][None, None, :] * hist_mapped[i]
        state = jnp.stack([jnp.clip(combined[0], lower, upper), combined[1]])
    return (state[0], state[1])


def solution(mesh):
    in_specs = (
        P("groups", "row"),
        P(("groups", "row"), None),
        P(("groups", "row"), None),
        P(("groups", "row")),
        P(("groups", "row"), None),
        P(("groups", "row"), None),
    )
    out_specs = (P(("groups", "row"), None), P(("groups", "row"), None))
    return jax.shard_map(
        per_device, mesh=mesh, in_specs=in_specs, out_specs=out_specs, check_vma=False
    )
```

profile of v0, /device:TPU:0, one launch (start us, length us, event | category | flops | bytes accessed | tf_op | source)
XLA Modules:
  0.0 811.2 jit_solution(4368304568969252268)
XLA Ops:
  19.6 50.7 %reduce-scatter.13.cloned.1.call-done = f32[32,128]{1,0:T(8,128)} async-done(((f32[512,128]{1,0:T(8,128)}), f32[32,128]{1,0:T(8,128)}) %reduce-scatter.13.cloned.1.call-update) | async-done | bytes 16400
  71.3 19.8 %all_gather.12 = bf16[512,128]{1,0:T(8,128)(2,1)S(1)} all-gather(bf16[32,128]{1,0:T(8,128)(2,1)S(1)} %copy.62), channel_id=1, replica_groups=mesh['groups'=2,'row'=16] {'row'}, dimensions={0}, use_global_device_ids=true | all-gather | bytes 139264 | tf_op jit(solution)/shard_map/all_gather | solution.py:65
  91.0 4.8 fusion.49
  97.9 29.8 %psum.28 = f32[1,1,128]{2,1,0:T(1,128)S(1)} all-reduce(f32[1,1,128]{2,1,0:T(1,128)S(1)} %bitcast.204), channel_id=1, replica_groups=mesh['groups'=2,'row'=16] {'row'}, use_global_device_ids=true, to_apply=%region_1.2 | all-reduce | flops 128 | bytes 1024 | tf_op jit(solution)/shard_map/psum | solution.py:82
  127.7 5.2 fusion.51
  143.1 49.9 %reduce-scatter.15.cloned.1.call-done = f32[32,128]{1,0:T(8,128)} async-done(((f32[512,128]{1,0:T(8,128)}), f32[32,128]{1,0:T(8,128)}) %reduce-scatter.15.cloned.1.call-update) | async-done | bytes 16400
  193.9 19.8 %all_gather.13 = bf16[512,128]{1,0:T(8,128)(2,1)S(1)} all-gather(bf16[32,128]{1,0:T(8,128)(2,1)S(1)} %copy.65), channel_id=1, replica_groups=mesh['groups'=2,'row'=16] {'row'}, dimensions={0}, use_global_device_ids=true | all-gather | bytes 139264 | tf_op jit(solution)/shard_map/all_gather | solution.py:65
  213.7 5.4 fusion.22
  228.1 75.1 %fusion.43 = f32[128,2,2]{2,1,0:T(2,128)S(1)} fusion(f32[2,2,4096,128]{2,3,1,0:T(8,128)S(1)} %pad_maximum_fusion.2), kind=kOutput, calls=%fused_computation.79 | convolution fusion | flops 50331648 | bytes 8390656 | tf_op jit(solution)/shard_map/icns,jcns->ijs/dot_general | solution.py:79
  303.4 29.8 %psum.29 = f32[2,2,128]{2,1,0:T(2,128)S(1)} all-reduce(f32[2,2,128]{2,1,0:T(2,128)S(1)} %bitcast.203), channel_id=1, replica_groups=mesh['groups'=2,'row'=16] {'row'}, use_global_device_ids=true, to_apply=%region_3.4 | all-reduce | flops 512 | bytes 4096 | tf_op jit(solution)/shard_map/psum | solution.py:82
  333.2 4.5 multiply_add_fusion.1
  347.9 49.9 %reduce-scatter.17.cloned.1.call-done = f32[32,128]{1,0:T(8,128)} async-done(((f32[512,128]{1,0:T(8,128)}), f32[32,128]{1,0:T(8,128)}) %reduce-scatter.17.cloned.1.call-update) | async-done | bytes 16400
  398.7 19.8 %all_gather.14 = bf16[512,128]{1,0:T(8,128)(2,1)S(1)} all-gather(bf16[32,128]{1,0:T(8,128)(2,1)S(1)} %copy.71), channel_id=1, replica_groups=mesh['groups'=2,'row'=16] {'row'}, dimensions={0}, use_global_device_ids=true | all-gather | bytes 139264 | tf_op jit(solution)/shard_map/all_gather | solution.py:65
  418.5 5.3 fusion.23
  432.0 9.3 %pad_maximum_fusion.1 = f32[3,2,4096,128]{2,3,1,0:T(8,128)} fusion(f32[1,2,4096,128]{2,3,1,0:T(8,128)} %maximum_subtract_fusion.1, f32[1,2,4096,128]{2,3,1,0:T(8,128)S(1)} %copy-done.14, f32[1,2,4096,128]{2,3,1,0:T(8,128)} %get-tuple-element.57), kind=kLoop, calls=%fused_computation.5 | loop fusion | flops 6291456 | bytes 25165824 | tf_op jit(solution)/shard_map/stack | solution.py:78
  441.2 102.3 %fusion.37 = f32[128,3,3]{2,1,0:T(4,128)S(1)} fusion(f32[3,2,4096,128]{2,3,1,0:T(8,128)} %pad_maximum_fusion.1), kind=kOutput, calls=%fused_computation.77 | convolution fusion | flops 113246208 | bytes 12587520 | tf_op jit(solution)/shard_map/icns,jcns->ijs/dot_general | solution.py:79
  543.6 30.3 %psum.30 = f32[3,3,128]{2,1,0:T(4,128)S(1)} all-reduce(f32[3,3,128]{2,1,0:T(4,128)S(1)} %bitcast.202), channel_id=1, replica_groups=mesh['groups'=2,'row'=16] {'row'}, use_global_device_ids=true, to_apply=%region_5.6 | all-reduce | flops 1152 | bytes 9216 | tf_op jit(solution)/shard_map/psum | solution.py:82
  574.1 5.4 multiply_add_fusion
  589.6 50.0 %reduce-scatter.19.cloned.1.call-done = f32[32,128]{1,0:T(8,128)} async-done(((f32[512,128]{1,0:T(8,128)}), f32[32,128]{1,0:T(8,128)}) %reduce-scatter.19.cloned.1.call-update) | async-done | bytes 16400
  640.4 19.8 %all_gather.15 = bf16[512,128]{1,0:T(8,128)(2,1)S(1)} all-gather(bf16[32,128]{1,0:T(8,128)(2,1)S(1)} %copy.77), channel_id=1, replica_groups=mesh['groups'=2,'row'=16] {'row'}, dimensions={0}, use_global_device_ids=true | all-gather | bytes 139264 | tf_op jit(solution)/shard_map/all_gather | solution.py:65
  660.2 5.4 fusion.24
  680.1 80.1 %fusion.40 = f32[128,4,4]{2,1,0:T(4,128)S(1)} fusion(f32[4,2,4096,128]{2,3,1,0:T(8,128)S(1)} %pad_maximum_fusion), kind=kOutput, calls=%fused_computation.78 | convolution fusion | flops 201326592 | bytes 16785408 | tf_op jit(solution)/shard_map/icns,jcns->ijs/dot_general | solution.py:79
  760.2 30.3 %psum.31 = f32[4,4,128]{2,1,0:T(4,128)S(1)} all-reduce(f32[4,4,128]{2,1,0:T(4,128)S(1)} %bitcast.201), channel_id=1, replica_groups=mesh['groups'=2,'row'=16] {'row'}, use_global_device_ids=true, to_apply=%region_7.8 | all-reduce | flops 2048 | bytes 16384 | tf_op jit(solution)/shard_map/psum | solution.py:82
  790.7 6.9 fusion.25
  (140 shorter events, 87.0 us)
Async XLA Ops:
  7.2 4.6 copy-start.34
  7.2 63.2 %reduce-scatter.13.cloned.1.call-start = ((), (), s32[]{:S(2)}) async-start(), calls=%async_computation.4 | async-start | bytes 278528
  11.8 181.2 %reduce-scatter.15.cloned.1.call-start = ((), (), s32[]{:S(2)}) async-start(), calls=%async_computation.5 | async-start | bytes 278528
  127.7 5.2 copy-start.3
  132.9 4.5 copy-start
  139.8 258.0 %reduce-scatter.17.cloned.1.call-start = ((), (), s32[]{:S(2)}) async-start(), calls=%async_computation.6 | async-start | bytes 278528
  213.7 5.4 copy-start.4
  219.7 3.7 copy-start.31
  223.4 3.7 copy-start.16
  224.1 4.1 copy-start.13
  333.2 4.5 copy-start.5
  337.8 4.5 copy-start.1
  344.7 294.9 %reduce-scatter.19.cloned.1.call-start = ((), (), s32[]{:S(2)}) async-start(), calls=%async_computation.7 | async-start | bytes 278528
  418.5 5.4 copy-start.6
  424.5 3.7 copy-start.32
  428.3 3.7 copy-start.14
  574.0 5.5 copy-start.7
  579.5 4.5 copy-start.2
  660.2 5.4 copy-start.8
  666.2 3.7 copy-start.30
  669.9 3.7 copy-start.15
  669.9 5.0 copy-start.17
  669.9 6.2 copy-start.22
  790.7 6.9 copy-start.9
  (15 other events, 32.6 us)
Sparse Core Ops, SparseCore 0:
  11.9 58.4 reduce-scatter.12
  139.9 52.9 reduce-scatter.14
  344.8 52.9 reduce-scatter.16
  586.5 52.9 reduce-scatter.18
where the time goes:
time: 819 us; the launch traced here: 811 us
  matrix products  287 us (35%)
  waiting for transfers between devices  201 us (25%)
  blocking collectives  200 us (24%)
  local copies, waits for them, and re-layouts  57.2 us (7%)
  other arithmetic  52.6 us (6%)
  between operations  14.5 us (2%)
    dot_general x3, matrix products, per_device(): jnp.einsum('icns,jcns->ijs', stacked, stacked, precision=lax.Precision.HI...  257 us
    unnamed x8, waiting for transfers between devices  201 us
    psum x4, blocking collectives, per_device(): whole = lax.psum(partial_all, 'row')  120 us
    all_gather x4, blocking collectives, per_device(): lax.all_gather(misfit, 'row', axis=0, tiled=True)  79.2 us
    unnamed x84, local copies, waits for them, and re-layouts  46.9 us
    dot_general x4, matrix products, per_device(): lax.dot_general(design_matrix, lax.all_gather(misfit, 'row', axis=0, tile...  20.9 us
    another operation x4, other arithmetic, per_device(): stacked = jnp.stack(hist_change)  19.4 us
    add x3, other arithmetic, per_device(): combined = combined + alpha[i][None, None, :] * hist_mapped[i]  16.8 us
  transfers between devices with their start and end apart: 4, of which 4 were waited for; matrix products, arithmetic and copies ran while one was open for 2% of the time, Pallas kernels for 0%

commit v1 on v0

v1 whole, which is shorter than its diff:
```python
import functools

import jax
import jax.numpy as jnp
from jax import lax
from jax.experimental import pallas as pl
from jax.experimental.pallas import tpu as pltpu
from jax.sharding import PartitionSpec as P

ITERS = 4

rho_plus_lip = 7.0


def solve_small(matrix, rhs):
    count = len(rhs)
    table = [list(line) for line in matrix]
    right = list(rhs)
    for p in range(count):
        for i in range(p + 1, count):
            factor = table[i][p] / table[p][p]
            for j in range(p, count):
                table[i][j] = table[i][j] - factor * table[p][j]
            right[i] = right[i] - factor * right[p]
    result = [None] * count
    for i in reversed(range(count)):
        total = right[i]
        for j in range(i + 1, count):
            total = total - table[i][j] * result[j]
        result[i] = total / table[i][i]
    return result


def mix_weights(gram):
    count = len(gram)
    trace = gram[0][0]
    for i in range(1, count):
        trace = trace + gram[i][i]
    shift = 0.01 * trace / count + 1e-06
    matrix = [[gram[i][j] + (shift if i == j else 0.0) for j in range(count)] for i in range(count)]
    solved = solve_small(matrix, [jnp.ones_like(trace)] * count)
    total = solved[0]
    for i in range(1, count):
        total = total + solved[i]
    return [item / total for item in solved]


def greet(n, me):
    barrier = pltpu.get_barrier_semaphore()
    for d in range(1, n):
        pl.semaphore_signal(
            barrier,
            inc=1,
            device_id={"row": lax.rem(me + d, n)},
            device_id_type=pl.DeviceIdType.MESH,
        )
    pl.semaphore_wait(barrier, n - 1)


def send(src, dst, send_sem, recv_sem, peer):
    copy = pltpu.make_async_remote_copy(
        src_ref=src,
        dst_ref=dst,
        send_sem=send_sem,
        recv_sem=recv_sem,
        device_id={"row": peer},
        device_id_type=pl.DeviceIdType.MESH,
    )
    copy.start()
    return copy


def spread(n, me, mine, whole, send_sem, recv_sem):
    copies = []
    for d in range(1, n):
        copies.append(
            send(mine, whole.at[me], send_sem.at[d], recv_sem.at[d], lax.rem(me + d, n))
        )
    whole[me] = mine[...]
    for copy in copies:
        copy.wait()


def first_misfit_kernel(n, targets_ref, out_ref, mine, whole, send_sem, recv_sem):
    me = lax.axis_index("row")
    mine[...] = (0.0 - targets_ref[...]).astype(jnp.bfloat16)
    greet(n, me)
    spread(n, me, mine, whole, send_sem, recv_sem)
    out_ref[...] = whole[...]


def misfit_kernel(
    n, product_ref, targets_ref, out_ref, slots, mine, whole, send_a, recv_a, send_b, recv_b
):
    me = lax.axis_index("row")
    greet(n, me)
    copies = []
    for d in range(1, n):
        peer = lax.rem(me + d, n)
        copies.append(
            send(product_ref.at[peer], slots.at[d - 1], send_a.at[d], recv_a.at[d], peer)
        )
    total = product_ref[me]
    for d in range(1, n):
        copies[d - 1].wait_recv()
        total = total + slots[d - 1]
    mine[...] = (total - targets_ref[...]).astype(jnp.bfloat16)
    spread(n, me, mine, whole, send_b, recv_b)
    for copy in copies:
        copy.wait_send()
    out_ref[...] = whole[...]


def gram_kernel(n, part_ref, out_ref, whole, send_sem, recv_sem):
    me = lax.axis_index("row")
    greet(n, me)
    spread(n, me, part_ref, whole, send_sem, recv_sem)
    total = whole[0]
    for i in range(1, n):
        total = total + whole[i]
    out_ref[...] = total


VMEM = pl.BlockSpec(memory_space=pltpu.VMEM)


def comm_params(number):
    return pltpu.CompilerParams(collective_id=number, has_side_effects=True)


def first_misfit(n, targets):
    kr, s = targets.shape
    out = pl.pallas_call(
        functools.partial(first_misfit_kernel, n),
        out_shape=jax.ShapeDtypeStruct((n, kr, s), jnp.bfloat16),
        in_specs=[VMEM],
        out_specs=VMEM,
        scratch_shapes=[
            pltpu.VMEM((kr, s), jnp.bfloat16),
            pltpu.VMEM((n, kr, s), jnp.bfloat16),
            pltpu.SemaphoreType.DMA((n,)),
            pltpu.SemaphoreType.DMA((n,)),
        ],
        compiler_params=comm_params(0),
        name="first_misfit",
    )(targets)
    return out.reshape(n * kr, s)


def next_misfit(n, product, targets):
    kr, s = targets.shape
    out = pl.pallas_call(
        functools.partial(misfit_kernel, n),
        out_shape=jax.ShapeDtypeStruct((n, kr, s), jnp.bfloat16),
        in_specs=[VMEM] * 2,
        out_specs=VMEM,
        scratch_shapes=[
            pltpu.VMEM((n - 1, kr, s), jnp.float32),
            pltpu.VMEM((kr, s), jnp.bfloat16),
            pltpu.VMEM((n, kr, s), jnp.bfloat16),
        ]
        + [pltpu.SemaphoreType.DMA((n,))] * 4,
        compiler_params=comm_params(1),
        name="next_misfit",
    )(product.reshape(n, kr, s), targets)
    return out.reshape(n * kr, s)


def sum_gram(n, part):
    return pl.pallas_call(
        functools.partial(gram_kernel, n),
        out_shape=jax.ShapeDtypeStruct(part.shape, part.dtype),
        in_specs=[VMEM],
        out_specs=VMEM,
        scratch_shapes=[
            pltpu.VMEM((n,) + part.shape, part.dtype),
            pltpu.SemaphoreType.DMA((n,)),
            pltpu.SemaphoreType.DMA((n,)),
        ],
        compiler_params=comm_params(2),
        name="sum_gram",
    )(part)


def bounds(lo_ref, hi_ref):
    return (
        lo_ref[...].astype(jnp.float32) * (1.0 / 64.0),
        hi_ref[...].astype(jnp.float32) * (1.0 / 64.0),
    )


def column_sum(x):
    return jnp.sum(x, axis=0, keepdims=True)


def start_kernel(a_ref, mis_ref, lin_ref, diag_ref, lo_ref, hi_ref, z_ref, u_ref, product_ref):
    lower, upper = bounds(lo_ref, hi_ref)
    gradient = lax.dot_general(
        a_ref[...], mis_ref[...], (((0,), (0,)), ((), ())), preferred_element_type=jnp.float32
    )
    gradient = gradient + lin_ref[...]
    moved = 0.0 - (1.0 / (rho_plus_lip + diag_ref[...])) * gradient
    boxed = jnp.minimum(jnp.maximum(moved, lower), upper)
    scaled = moved - boxed
    z_ref[...] = boxed
    u_ref[...] = scaled
    add = jnp.dot(
        a_ref[...], (boxed - scaled).astype(jnp.bfloat16), preferred_element_type=jnp.float32
    )

    @pl.when(pl.program_id(0) == 0)
    def _():
        product_ref[...] = jnp.zeros_like(product_ref)

    product_ref[...] += add


def map_kernel(iteration, *refs):
    a_ref, mis_ref, lin_ref, diag_ref, lo_ref, hi_ref, z_ref, u_ref = refs[:8]
    rest = refs[8:]
    if iteration == 1:
        prior = [(z_ref, u_ref)]
    else:
        prior = [(rest[2 * i], rest[2 * i + 1]) for i in range(iteration)]
        rest = rest[2 * iteration:]
    mz_ref, mu_ref = rest[:2]
    gram_ref = rest[-1]
    lower, upper = bounds(lo_ref, hi_ref)
    z, u = z_ref[...], u_ref[...]
    point = z - u
    diagonal = diag_ref[...]
    gradient = lax.dot_general(
        a_ref[...], mis_ref[...], (((0,), (0,)), ((), ())), preferred_element_type=jnp.float32
    )
    gradient = gradient + diagonal * point + lin_ref[...]
    moved = point - (1.0 / (rho_plus_lip + diagonal)) * gradient
    boxed = jnp.minimum(jnp.maximum(moved + u, lower), upper)
    scaled = u + moved - boxed
    mz_ref[...] = boxed
    mu_ref[...] = scaled
    cz, cu = boxed - z, scaled - u
    if iteration < ITERS - 1:
        rest[2][...] = cz
        rest[3][...] = cu
    rows = [column_sum(cz * pz[...] + cu * pu[...]) for pz, pu in prior]
    rows.append(column_sum(cz * cz + cu * cu))
    if iteration == 1:
        rows.append(column_sum(z * z + u * u))

    @pl.when(pl.program_id(0) == 0)
    def _():
        gram_ref[...] = jnp.zeros_like(gram_ref)

    for i, row in enumerate(rows):
        gram_ref[i:i + 1, :] += row


def mix_kernel(iteration, *refs):
    count = iteration + 1
    grams, refs = refs[:iteration], refs[iteration:]
    lo_ref, hi_ref = refs[:2]
    mapped = [(refs[2 + 2 * i], refs[3 + 2 * i]) for i in range(count)]
    refs = refs[2 + 2 * count:]
    last = iteration == ITERS - 1
    if last:
        z_ref, u_ref, alpha_ref = refs
    else:
        a_ref, z_ref, u_ref, product_ref, alpha_ref = refs

    @pl.when(pl.program_id(0) == 0)
    def _():
        gram = [[None] * count for _ in range(count)]
        gram[0][0] = grams[0][2:3, :]
        for i in range(1, count):
            for j in range(i + 1):
                gram[i][j] = gram[j][i] = grams[i - 1][j:j + 1, :]
        for i, row in enumerate(mix_weights(gram)):
            alpha_ref[i:i + 1, :] = row
        if not last:
            product_ref[...] = jnp.zeros_like(product_ref)

    lower, upper = bounds(lo_ref, hi_ref)
    z = alpha_ref[0:1, :] * mapped[0][0][...]
    u = alpha_ref[0:1, :] * mapped[0][1][...]
    for i in range(1, count):
        z = z + alpha_ref[i:i + 1, :] * mapped[i][0][...]
        u = u + alpha_ref[i:i + 1, :] * mapped[i][1][...]
    z = jnp.minimum(jnp.maximum(z, lower), upper)
    z_ref[...] = z
    u_ref[...] = u
    if not last:
        product_ref[...] += jnp.dot(
            a_ref[...], (z - u).astype(jnp.bfloat16), preferred_element_type=jnp.float32
        )


def per_device(n, design_matrix, targets, linear, diagonal, lower_code, upper_code):
    k, local = design_matrix.shape
    s = linear.shape[1]
    block = min(512, local)
    grid = (local // block,)
    tile = pl.BlockSpec((block, s), lambda i: (i, 0))
    a_spec = pl.BlockSpec((k, block), lambda i: (0, i))
    d_spec = pl.BlockSpec((block, 1), lambda i: (i, 0))
    k_spec = pl.BlockSpec((k, s), lambda i: (0, 0))
    g_spec = pl.BlockSpec((8, s), lambda i: (0, 0))
    big = jax.ShapeDtypeStruct((local, s), jnp.float32)
    tall = jax.ShapeDtypeStruct((k, s), jnp.float32)
    small = jax.ShapeDtypeStruct((8, s), jnp.float32)
    params = pltpu.CompilerParams(dimension_semantics=("arbitrary",))
    diag = diagonal[:, None]

    misfit = first_misfit(n, targets)
    z, u, product = pl.pallas_call(
        start_kernel,
        grid=grid,
        in_specs=[a_spec, k_spec, tile, d_spec, tile, tile],
        out_specs=[tile, tile, k_spec],
        out_shape=[big, big, tall],
        compiler_params=params,
        name="start",
    )(design_matrix, misfit, linear, diag, lower_code, upper_code)
    mapped = [z, u]
    changes = [z, u]
    grams = []
    for iteration in range(1, ITERS):
        last = iteration == ITERS - 1
        misfit = next_misfit(n, product, targets)
        prior = changes if iteration > 1 else []
        out = pl.pallas_call(
            functools.partial(map_kernel, iteration),
            grid=grid,
            in_specs=[a_spec, k_spec, tile, d_spec] + [tile] * (4 + len(prior)),
            out_specs=[tile] * (2 if last else 4) + [g_spec],
            out_shape=[big] * (2 if last else 4) + [small],
            compiler_params=params,
            name="map",
        )(design_matrix, misfit, linear, diag, lower_code, upper_code, z, u, *prior)
        mapped = mapped + list(out[:2])
        changes = changes + list(out[2:-1])
        grams.append(sum_gram(n, out[-1]))
        out = pl.pallas_call(
            functools.partial(mix_kernel, iteration),
            grid=grid,
            in_specs=[g_spec] * iteration
            + [tile] * (2 + len(mapped))
            + ([] if last else [a_spec]),
            out_specs=[tile, tile] + ([] if last else [k_spec]),
            out_shape=[big, big] + ([] if last else [tall]),
            scratch_shapes=[pltpu.VMEM((8, s), jnp.float32)],
            compiler_params=params,
            name="mix",
        )(*grams, lower_code, upper_code, *mapped, *([] if last else [design_matrix]))
        if last:
            z, u = out
        else:
            z, u, product = out
    return z, u


def solution(mesh):
    in_specs = (
        P("groups", "row"),
        P(("groups", "row"), None),
        P(("groups", "row"), None),
        P(("groups", "row")),
        P(("groups", "row"), None),
        P(("groups", "row"), None),
    )
    out_specs = (P(("groups", "row"), None), P(("groups", "row"), None))
    return jax.shard_map(
        functools.partial(per_device, mesh.shape["row"]),
        mesh=mesh,
        in_specs=in_specs,
        out_specs=out_specs,
        check_vma=False,
    )
```

time: 819 us -> 176 us (0.21)
  matrix products: 287 us -> 0 us
  waiting for transfers between devices: 201 us -> 0 us
  blocking collectives: 200 us -> 0 us
  Pallas kernels: 0 us -> 171 us
  local copies, waits for them, and re-layouts: 57.2 us -> 2.68 us
  other arithmetic: 52.6 us -> 0 us
  between operations: 14.5 us -> 0.71 us
    dot_general x11 -> x0, matrix products: 287 us -> none  [the longest x3 257 us: per_device(): jnp.einsum('icns,jcns->ijs', stacked, stacked, precision=lax.Precision.HI...]
    unnamed x8 -> x0, waiting for transfers between devices: 201 us -> none
    pallas_call x0 -> x14, Pallas kernels: none -> 171 us  [the longest x3 53.4 us: next_misfit(): pl.pallas_call(functools.partial(misfit_kernel, n), out_shape=jax.ShapeDt...]
    psum x4 -> x0, blocking collectives: 120 us -> none  [per_device(): whole = lax.psum(partial_all, 'row')]
    all_gather x4 -> x0, blocking collectives: 79.2 us -> none  [per_device(): lax.all_gather(misfit, 'row', axis=0, tiled=True)]
    unnamed x84 -> x0, local copies, waits for them, and re-layouts: 46.9 us -> none
    another operation x10 -> x0, other arithmetic: 26 us -> none  [the longest x4 19.4 us: per_device(): stacked = jnp.stack(hist_change)]
    add x3 -> x0, other arithmetic: 16.8 us -> none  [per_device(): combined = combined + alpha[i][None, None, :] * hist_mapped[i]]
  transfers between devices with their start and end apart: 4 -> 0, of which waited for: 4 -> 0; matrix products, arithmetic and copies ran while one was open for 2% -> 0% of each run, Pallas kernels for 0% -> 0%
where the time goes in v1:
time: 176 us; the launch traced here: 175 us
  Pallas kernels  171 us (97%)
  local copies, waits for them, and re-layouts  2.68 us (2%)
    pallas_call x3, Pallas kernels, next_misfit(): pl.pallas_call(functools.partial(misfit_kernel, n), out_shape=jax.ShapeDt...  53.4 us
    pallas_call x3, Pallas kernels, per_device(): pl.pallas_call(functools.partial(map_kernel, iteration), grid=grid, in_sp...  40.6 us
    pallas_call x3, Pallas kernels, per_device(): pl.pallas_call(functools.partial(mix_kernel, iteration), grid=grid, in_sp...  31.5 us
    pallas_call x3, Pallas kernels, sum_gram(): pl.pallas_call(functools.partial(gram_kernel, n), out_shape=jax.ShapeDtyp...  23.8 us
    pallas_call x1, Pallas kernels, per_device(): pl.pallas_call(start_kernel, grid=grid, in_specs=[a_spec, k_spec, tile, d...  11.4 us
    pallas_call x1, Pallas kernels, first_misfit(): pl.pallas_call(functools.partial(first_misfit_kernel, n), out_shape=jax.S...  10.7 us

profile of v1, /device:TPU:0, one launch (start us, length us, event | category | flops | bytes accessed | tf_op | source)
XLA Modules:
  0.0 174.8 jit_solution(12469121234268170336)
XLA Ops:
  0.6 10.7 %first_misfit.1 = bf16[16,32,128]{2,1,0:T(8,128)(2,1)} custom-call(f32[32,128]{1,0:T(8,128)} %targets_ref.7), custom_call_target="tpu_custom_call" | custom-call | tf_op jit(solution)/shard_map/first_misfit/pallas_call | solution.py:133
  11.3 2.7 %copy.8.diag_ref.refs_3_ = f32[4096,1]{1,0:T(8,128)} copy(f32[4096,1]{0,1:T(1,128)} %bitcast.15) | data formatting | bytes 32768 | tf_op jit(solution)/shard_map/broadcast_in_dim | solution.py:311
  14.0 11.4 %start.1 = (f32[4096,128]{1,0:T(8,128)}, f32[4096,128]{1,0:T(8,128)}, f32[512,128]{1,0:T(8,128)}) custom-call(bf16[512,4096]{1,0:T(8,128)(2,1)} %refs_0_.5, bf16[512,128]{1,0:T(8,128)(2,1)} %bitcast.11, f32[4096,128]{1,0:T(8,128)} %refs_2_.9, f32[4096,1]{1,0:T(8,128)} %copy.8.diag_ref.refs_3_, s32[4096,128]{1,0:T(8,128)} %refs_3_.3, s32[4096,128]{1,0:T(8,128)} %refs_4_.7), custom_call_target="tpu_custom_call" | custom-call | tf_op jit(solution)/shard_map/start/pallas_call | solution.py:314
  25.4 19.0 %next_misfit.3 = bf16[16,32,128]{2,1,0:T(8,128)(2,1)} custom-call(f32[16,32,128]{2,1,0:T(8,128)} %bitcast.12, f32[32,128]{1,0:T(8,128)} %targets_ref.7), custom_call_target="tpu_custom_call" | custom-call | tf_op jit(solution)/shard_map/next_misfit/pallas_call | solution.py:152
  44.4 12.4 %map.3 = (f32[4096,128]{1,0:T(8,128)}, f32[4096,128]{1,0:T(8,128)}, f32[4096,128]{1,0:T(8,128)}, f32[4096,128]{1,0:T(8,128)}, f32[8,128]{1,0:T(8,128)}) custom-call(bf16[512,4096]{1,0:T(8,128)(2,1)} %refs_0_.5, bf16[512,128]{1,0:T(8,128)(2,1)} %bitcast.10, f32[4096,128]{1,0:T(8,128)} %refs_2_.9, f32[4096,1]{1,0:T(8,128)} %copy.8.diag_ref.refs_3_, ...), custom_call_target="tpu_custom_call" | custom-call | tf_op jit(solution)/shard_map/map/pallas_call | solution.py:330
  56.8 7.9 %sum_gram.3.refs_0_ = f32[8,128]{1,0:T(8,128)} custom-call(f32[8,128]{1,0:T(8,128)} %get-tuple-element.27.part_ref), custom_call_target="tpu_custom_call" | custom-call | tf_op jit(solution)/shard_map/sum_gram/pallas_call | solution.py:170
  64.8 9.9 %mix.3 = (f32[4096,128]{1,0:T(8,128)}, f32[4096,128]{1,0:T(8,128)}, f32[512,128]{1,0:T(8,128)}) custom-call(f32[8,128]{1,0:T(8,128)} %sum_gram.3.refs_0_, s32[4096,128]{1,0:T(8,128)} %refs_3_.3, s32[4096,128]{1,0:T(8,128)} %refs_4_.7, f32[4096,128]{1,0:T(8,128)} %get-tuple-element.25.refs_6_.refs_3_.refs_8_.refs_4_.refs_5_, ...), custom_call_target="tpu_custom_call" | custom-call | tf_op jit(solution)/shard_map/mix/pallas_call | solution.py:342
  74.7 17.0 %next_misfit.4 = bf16[16,32,128]{2,1,0:T(8,128)(2,1)} custom-call(f32[16,32,128]{2,1,0:T(8,128)} %bitcast.13, f32[32,128]{1,0:T(8,128)} %targets_ref.7), custom_call_target="tpu_custom_call" | custom-call | tf_op jit(solution)/shard_map/next_misfit/pallas_call | solution.py:152
  91.7 14.5 %map.4 = (f32[4096,128]{1,0:T(8,128)}, f32[4096,128]{1,0:T(8,128)}, f32[4096,128]{1,0:T(8,128)}, f32[4096,128]{1,0:T(8,128)}, f32[8,128]{1,0:T(8,128)}) custom-call(bf16[512,4096]{1,0:T(8,128)(2,1)} %refs_0_.5, bf16[512,128]{1,0:T(8,128)(2,1)} %bitcast.9, f32[4096,128]{1,0:T(8,128)} %refs_2_.9, f32[4096,1]{1,0:T(8,128)} %copy.8.diag_ref.refs_3_, ...), custom_call_target="tpu_custom_call" | custom-call | tf_op jit(solution)/shard_map/map/pallas_call | solution.py:330
  106.2 7.9 %sum_gram.4.refs_1_ = f32[8,128]{1,0:T(8,128)} custom-call(f32[8,128]{1,0:T(8,128)} %get-tuple-element.35.part_ref), custom_call_target="tpu_custom_call" | custom-call | tf_op jit(solution)/shard_map/sum_gram/pallas_call | solution.py:170
  114.1 11.1 %mix.4 = (f32[4096,128]{1,0:T(8,128)}, f32[4096,128]{1,0:T(8,128)}, f32[512,128]{1,0:T(8,128)}) custom-call(f32[8,128]{1,0:T(8,128)} %sum_gram.3.refs_0_, f32[8,128]{1,0:T(8,128)} %sum_gram.4.refs_1_, s32[4096,128]{1,0:T(8,128)} %refs_3_.3, s32[4096,128]{1,0:T(8,128)} %refs_4_.7, f32[4096,128]{1,0:T(8,128)} %get-tuple-element.25.refs_6_.refs_3_.refs_8_.refs_4_.refs_5_, ...), custom_call_target="tpu_custom_call" | custom-call | tf_op jit(solution)/shard_map/mix/pallas_call | solution.py:342
  125.2 17.4 %next_misfit.5 = bf16[16,32,128]{2,1,0:T(8,128)(2,1)} custom-call(f32[16,32,128]{2,1,0:T(8,128)} %bitcast.14, f32[32,128]{1,0:T(8,128)} %targets_ref.7), custom_call_target="tpu_custom_call" | custom-call | tf_op jit(solution)/shard_map/next_misfit/pallas_call | solution.py:152
  142.6 13.7 %map.5 = (f32[4096,128]{1,0:T(8,128)}, f32[4096,128]{1,0:T(8,128)}, f32[8,128]{1,0:T(8,128)}) custom-call(bf16[512,4096]{1,0:T(8,128)(2,1)} %refs_0_.5, bf16[512,128]{1,0:T(8,128)(2,1)} %bitcast.8, f32[4096,128]{1,0:T(8,128)} %refs_2_.9, f32[4096,1]{1,0:T(8,128)} %copy.8.diag_ref.refs_3_, s32[4096,128]{1,0:T(8,128)} %refs_3_.3, s32[4096,128]{1,0:T(8,128)} %refs_4_.7, ...), custom_call_target="tpu_custom_call" | custom-call | tf_op jit(solution)/shard_map/map/pallas_call | solution.py:330
  156.3 7.9 %sum_gram.5.refs_2_ = f32[8,128]{1,0:T(8,128)} custom-call(f32[8,128]{1,0:T(8,128)} %get-tuple-element.43.part_ref), custom_call_target="tpu_custom_call" | custom-call | tf_op jit(solution)/shard_map/sum_gram/pallas_call | solution.py:170
  164.3 10.5 %mix.5 = (f32[4096,128]{1,0:T(8,128)}, f32[4096,128]{1,0:T(8,128)}) custom-call(f32[8,128]{1,0:T(8,128)} %sum_gram.3.refs_0_, f32[8,128]{1,0:T(8,128)} %sum_gram.4.refs_1_, f32[8,128]{1,0:T(8,128)} %sum_gram.5.refs_2_, s32[4096,128]{1,0:T(8,128)} %refs_3_.3, s32[4096,128]{1,0:T(8,128)} %refs_4_.7, ...), custom_call_target="tpu_custom_call" | custom-call | tf_op jit(solution)/shard_map/mix/pallas_call | solution.py:342

commit v2 on v0

v2 whole, which is shorter than its diff:
```python
import functools

import jax
import jax.numpy as jnp
from jax import lax
from jax.experimental import pallas as pl
from jax.experimental.pallas import tpu as pltpu
from jax.sharding import PartitionSpec as P

ITERS = 4
TERM = jnp.float32

rho_plus_lip = 7.0


def solve_small(matrix, rhs):
    count = len(rhs)
    table = [list(line) for line in matrix]
    right = list(rhs)
    for p in range(count):
        for i in range(p + 1, count):
            factor = table[i][p] / table[p][p]
            for j in range(p, count):
                table[i][j] = table[i][j] - factor * table[p][j]
            right[i] = right[i] - factor * right[p]
    result = [None] * count
    for i in reversed(range(count)):
        total = right[i]
        for j in range(i + 1, count):
            total = total - table[i][j] * result[j]
        result[i] = total / table[i][i]
    return result


def mix_weights(gram):
    count = len(gram)
    trace = gram[0][0]
    for i in range(1, count):
        trace = trace + gram[i][i]
    shift = 0.01 * trace / count + 1e-06
    matrix = [[gram[i][j] + (shift if i == j else 0.0) for j in range(count)] for i in range(count)]
    solved = solve_small(matrix, [jnp.ones_like(trace)] * count)
    total = solved[0]
    for i in range(1, count):
        total = total + solved[i]
    return [item / total for item in solved]


def greet(n, me):
    barrier = pltpu.get_barrier_semaphore()
    for d in range(1, n):
        pl.semaphore_signal(
            barrier,
            inc=1,
            device_id={"row": lax.rem(me + d, n)},
            device_id_type=pl.DeviceIdType.MESH,
        )
    pl.semaphore_wait(barrier, n - 1)


def send(src, dst, send_sem, recv_sem, peer):
    copy = pltpu.make_async_remote_copy(
        src_ref=src,
        dst_ref=dst,
        send_sem=send_sem,
        recv_sem=recv_sem,
        device_id={"row": peer},
        device_id_type=pl.DeviceIdType.MESH,
    )
    copy.start()
    return copy


def spread(n, me, mine, whole, send_sem, recv_sem):
    copies = []
    for d in range(1, n):
        copies.append(
            send(mine, whole.at[me], send_sem.at[d], recv_sem.at[d], lax.rem(me + d, n))
        )
    whole[me] = mine[...]
    for copy in copies:
        copy.wait()


def chunks(local, size, body):
    def step(i, carry):
        body(pl.ds(pl.multiple_of(i * size, size), size))
        return carry

    lax.fori_loop(0, local // size, step, 0)


def column_sum(x):
    return jnp.sum(x, axis=0, keepdims=True)


def clip_codes(x, lo_ref, hi_ref, at):
    lower = lo_ref[at, :].astype(jnp.float32) * (1.0 / 64.0)
    upper = hi_ref[at, :].astype(jnp.float32) * (1.0 / 64.0)
    return jnp.minimum(jnp.maximum(x, lower), upper)


def whole_kernel(
    n,
    size,
    a_ref,
    targets_ref,
    lin_ref,
    diag_ref,
    lo_ref,
    hi_ref,
    z_ref,
    u_ref,
    mapped,
    changes,
    acc,
    terms,
    slots,
    mine,
    misfits,
    part,
    parts,
    grams,
    alpha_ref,
    send_a,
    recv_a,
    send_b,
    recv_b,
    send_c,
    recv_c,
):
    me = lax.axis_index("row")
    local = lin_ref.shape[0]
    k = a_ref.shape[0]

    def gradient_of(at):
        return lax.dot_general(
            a_ref[:, at],
            misfits[...].reshape(k, -1),
            (((0,), (0,)), ((), ())),
            preferred_element_type=jnp.float32,
        )

    def add_product(at, point):
        acc[...] += jnp.dot(
            a_ref[:, at], point.astype(jnp.bfloat16), preferred_element_type=jnp.float32
        )

    mine[...] = (0.0 - targets_ref[...]).astype(jnp.bfloat16)
    greet(n, me)
    spread(n, me, mine, misfits, send_b, recv_b)
    acc[...] = jnp.zeros_like(acc)
    part[...] = jnp.zeros_like(part)

    def start(at):
        gradient = gradient_of(at) + lin_ref[at, :]
        moved = 0.0 - (1.0 / (rho_plus_lip + diag_ref[at, :])) * gradient
        boxed = clip_codes(moved, lo_ref, hi_ref, at)
        scaled = moved - boxed
        mapped[0, 0, at, :] = boxed
        mapped[0, 1, at, :] = scaled
        part[7:8, :] += column_sum(boxed * boxed + scaled * scaled)
        add_product(at, boxed - scaled)

    chunks(local, size, start)

    for iteration in range(1, ITERS):
        count = iteration + 1
        last = iteration == ITERS - 1
        terms[...] = acc[...].reshape(terms.shape).astype(terms.dtype)
        copies = []
        for d in range(1, n):
            peer = lax.rem(me + d, n)
            copies.append(
                send(terms.at[peer], slots.at[d - 1], send_a.at[d], recv_a.at[d], peer)
            )
        total = terms[me].astype(jnp.float32)
        for d in range(1, n):
            copies[d - 1].wait_recv()
            total = total + slots[d - 1].astype(jnp.float32)
        mine[...] = (total - targets_ref[...]).astype(jnp.bfloat16)
        spread(n, me, mine, misfits, send_b, recv_b)
        for copy in copies:
            copy.wait_send()
        if iteration > 1:
            part[...] = jnp.zeros_like(part)

        def advance(at):
            if iteration == 1:
                z, u = mapped[0, 0, at, :], mapped[0, 1, at, :]
            else:
                z, u = z_ref[at, :], u_ref[at, :]
            point = z - u
            diagonal = diag_ref[at, :]
            gradient = gradient_of(at) + diagonal * point + lin_ref[at, :]
            moved = point - (1.0 / (rho_plus_lip + diagonal)) * gradient
            boxed = clip_codes(moved + u, lo_ref, hi_ref, at)
            scaled = u + moved - boxed
            mapped[iteration, 0, at, :] = boxed
            mapped[iteration, 1, at, :] = scaled
            cz, cu = boxed - z, scaled - u
            if not last:
                changes[iteration - 1, 0, at, :] = cz
                changes[iteration - 1, 1, at, :] = cu
            part[0:1, :] += column_sum(cz * mapped[0, 0, at, :] + cu * mapped[0, 1, at, :])
            for i in range(1, iteration):
                part[i:i + 1, :] += column_sum(
                    cz * changes[i - 1, 0, at, :] + cu * changes[i - 1, 1, at, :]
                )
            part[iteration:count, :] += column_sum(cz * cz + cu * cu)

        chunks(local, size, advance)

        spread(n, me, part, parts, send_c, recv_c)
        whole = parts[0]
        for i in range(1, n):
            whole = whole + parts[i]
        grams[iteration - 1] = whole

        gram = [[None] * count for _ in range(count)]
        gram[0][0] = grams[0, 7:8, :]
        for i in range(1, count):
            for j in range(i + 1):
                gram[i][j] = gram[j][i] = grams[i - 1, j:j + 1, :]
        for i, row in enumerate(mix_weights(gram)):
            alpha_ref[i:i + 1, :] = row
        acc[...] = jnp.zeros_like(acc)

        def mix(at):
            z = alpha_ref[0:1, :] * mapped[0, 0, at, :]
            u = alpha_ref[0:1, :] * mapped[0, 1, at, :]
            for i in range(1, count):
                z = z + alpha_ref[i:i + 1, :] * mapped[i, 0, at, :]
                u = u + alpha_ref[i:i + 1, :] * mapped[i, 1, at, :]
            z = clip_codes(z, lo_ref, hi_ref, at)
            z_ref[at, :] = z
            u_ref[at, :] = u
            if not last:
                add_product(at, z - u)

        chunks(local, size, mix)


def per_device(n, design_matrix, targets, linear, diagonal, lower_code, upper_code):
    k = design_matrix.shape[0]
    local, s = linear.shape
    kr = k // n
    big = jax.ShapeDtypeStruct((local, s), jnp.float32)
    vmem = pl.BlockSpec(memory_space=pltpu.VMEM)
    dma = pltpu.SemaphoreType.DMA((n,))
    return pl.pallas_call(
        functools.partial(whole_kernel, n, min(512, local)),
        in_specs=[vmem] * 6,
        out_specs=[vmem] * 2,
        out_shape=[big, big],
        scratch_shapes=[
            pltpu.VMEM((ITERS, 2, local, s), jnp.float32),
            pltpu.VMEM((ITERS - 2, 2, local, s), jnp.float32),
            pltpu.VMEM((k, s), jnp.float32),
            pltpu.VMEM((n, kr, s), TERM),
            pltpu.VMEM((n - 1, kr, s), TERM),
            pltpu.VMEM((kr, s), jnp.bfloat16),
            pltpu.VMEM((n, kr, s), jnp.bfloat16),
            pltpu.VMEM((8, s), jnp.float32),
            pltpu.VMEM((n, 8, s), jnp.float32),
            pltpu.VMEM((ITERS - 1, 8, s), jnp.float32),
            pltpu.VMEM((8, s), jnp.float32),
        ]
        + [dma] * 6,
        compiler_params=pltpu.CompilerParams(
            collective_id=0, has_side_effects=True, vmem_limit_bytes=60 * 1024 * 1024
        ),
        name="whole",
    )(design_matrix, targets, linear, diagonal[:, None], lower_code, upper_code)


def solution(mesh):
    in_specs = (
        P("groups", "row"),
        P(("groups", "row"), None),
        P(("groups", "row"), None),
        P(("groups", "row")),
        P(("groups", "row"), None),
        P(("groups", "row"), None),
    )
    out_specs = (P(("groups", "row"), None), P(("groups", "row"), None))
    return jax.shard_map(
        functools.partial(per_device, mesh.shape["row"]),
        mesh=mesh,
        in_specs=in_specs,
        out_specs=out_specs,
        check_vma=False,
    )
```

time: 819 us -> 105 us (0.13)
  matrix products: 287 us -> 0 us
  waiting for transfers between devices: 201 us -> 0 us
  blocking collectives: 200 us -> 0 us
  Pallas kernels: 0 us -> 96.4 us
  other arithmetic: 52.6 us -> 0 us
  local copies, waits for them, and re-layouts: 57.2 us -> 7.2 us
  between operations: 14.5 us -> 0.65 us
    dot_general x11 -> x0, matrix products: 287 us -> none  [the longest x3 257 us: per_device(): jnp.einsum('icns,jcns->ijs', stacked, stacked, precision=lax.Precision.HI...]
    unnamed x8 -> x0, waiting for transfers between devices: 201 us -> none
    psum x4 -> x0, blocking collectives: 120 us -> none  [per_device(): whole = lax.psum(partial_all, 'row')]
    pallas_call x0 -> x1, Pallas kernels: none -> 96.4 us  [per_device(): pl.pallas_call(functools.partial(whole_kernel, n, min(512, local)), in_sp...]
    all_gather x4 -> x0, blocking collectives: 79.2 us -> none  [per_device(): lax.all_gather(misfit, 'row', axis=0, tiled=True)]
    unnamed x84 -> x4, local copies, waits for them, and re-layouts: 46.9 us -> 4.52 us
    another operation x10 -> x0, other arithmetic: 26 us -> none  [the longest x4 19.4 us: per_device(): stacked = jnp.stack(hist_change)]
    add x3 -> x0, other arithmetic: 16.8 us -> none  [per_device(): combined = combined + alpha[i][None, None, :] * hist_mapped[i]]
  transfers between devices with their start and end apart: 4 -> 0, of which waited for: 4 -> 0; matrix products, arithmetic and copies ran while one was open for 2% -> 0% of each run, Pallas kernels for 0% -> 0%
where the time goes in v2:
time: 105 us; the launch traced here: 104 us
  Pallas kernels  96.4 us (92%)
  local copies, waits for them, and re-layouts  7.2 us (7%)
    pallas_call x1, Pallas kernels, per_device(): pl.pallas_call(functools.partial(whole_kernel, n, min(512, local)), in_sp...  96.4 us
    unnamed x4, local copies, waits for them, and re-layouts  4.52 us
    broadcast_in_dim x1, local copies, waits for them, and re-layouts, per_device(): diagonal[:, None]  2.68 us

profile of v2, /device:TPU:0, one launch (start us, length us, event | category | flops | bytes accessed | tf_op | source)
XLA Modules:
  0.0 104.3 jit_solution(10110151814883812473)
XLA Ops:
  0.6 2.7 %copy.8.diag_ref = f32[4096,1]{1,0:T(8,128)} copy(f32[4096,1]{0,1:T(1,128)} %bitcast.1) | data formatting | bytes 32768 | tf_op jit(solution)/shard_map/broadcast_in_dim | solution.py:274
  3.3 96.4 %whole.1 = (f32[4096,128]{1,0:T(8,128)}, f32[4096,128]{1,0:T(8,128)}) custom-call(bf16[512,4096]{1,0:T(8,128)(2,1)} %a_ref.1, f32[32,128]{1,0:T(8,128)} %targets_ref.1, f32[4096,128]{1,0:T(8,128)} %lin_ref.1, f32[4096,1]{1,0:T(8,128)} %copy.8.diag_ref, s32[4096,128]{1,0:T(8,128)} %lo_ref.1, s32[4096,128]{1,0:T(8,128)} %hi_ref.1), custom_call_target="tpu_custom_call" | custom-call | tf_op jit(solution)/shard_map/whole/pallas_call | solution.py:251
  99.8 0.0 copy-start
  99.8 3.2 %copy.11 = f32[4096,128]{1,0:T(8,128)} copy(f32[4096,128]{1,0:T(8,128)} %get-tuple-element.4) | data formatting | bytes 4194304
  103.0 0.0 copy-done
  103.0 1.3 %copy.12 = f32[4096,128]{1,0:T(8,128)} copy(f32[4096,128]{1,0:T(8,128)S(1)} %copy-done) | data formatting | bytes 4194304
Async XLA Ops:
  99.8 3.2 %copy-start = (f32[4096,128]{1,0:T(8,128)S(1)}, f32[4096,128]{1,0:T(8,128)}, u32[]{:S(2)}) copy-start(f32[4096,128]{1,0:T(8,128)} %get-tuple-element.5) | copy-start | bytes 6291460
